TPU v7x, 128 devices: a whole 4x4x4 slice. The times are simulated.
128 devices in a mesh: lon: 8 (over z, y_hi), lat: 16 (over y_lo, x, core).
Axes of the slice: x: 4, y: 4 (y_hi: 2, y_lo: 2; y = y_hi * 2 + y_lo), z: 4, core: 2. Of those that a mesh axis runs over, the one named last changes fastest.
Arguments:
- atmos_state: bfloat16 [512, 512, 256], P('lat', 'lon'), may hold values from -6 to 6
- atmos_weights: bfloat16 [9, 256, 256], replicated, may hold values from -0.125 to 0.125
- flux_project: bfloat16 [256, 64], replicated, may hold values from -0.75 to 0.75
- source_row: int32 [512, 512, 4], P('lat', 'lon'), may hold values from 0 to 511, as said below
- source_col: int32 [512, 512, 4], P('lat', 'lon'), may hold values from 0 to 511, as said below
- intersection_weight: float32 [512, 512, 4], P('lat', 'lon'), may hold values from 0 to 1
- ocean_state: bfloat16 [512, 512, 256], P('lat', 'lon'), may hold values from -6 to 6
- flux_inject: bfloat16 [64, 256], replicated, may hold values from -0.75 to 0.75
- ocean_mask: int32 [512, 512], P('lat', 'lon'), may hold values 0 or 1
- ocean_weights: bfloat16 [9, 256, 256], replicated, may hold values from -0.125 to 0.125
- out_cotangent: bfloat16 [512, 512, 256], P('lat', 'lon'), may hold values from -6 to 6
Outputs:
- ocean_out: bfloat16 [512, 512, 256], P('lat', 'lon')
- grad_atmos: float32 [9, 256, 256], replicated
- grad_ocean: float32 [9, 256, 256], replicated
- grad_project: float32 [256, 64], replicated
- grad_inject: float32 [64, 256], replicated
Inputs may be any that keep to these rules, and one draw needn't show every extreme that they name: `source_row`: entry k of ocean cell (j, i) names an atmosphere row within 2 rows of j; for ocean rows j >= 512 - 32 (the band beside the fold) within 32 rows of j; both reaches are attained. `source_col`: entry k of ocean cell (j, i) names an atmosphere column within 2 columns of i, counted cyclically; for ocean rows j >= 480 within 64 columns of i; both reaches are attained.
All inputs are finite; a program needn't handle non-finite values. No bound on the sum of `ocean_mask` on one device may be relied on, other than what follows from the above.
Results may differ from a plain program's by a relative error of at most 0.018.
Values may be sent and summed in bfloat16 or wider, within the bound.
No kernel may reach another device: no remote copies, remote signals or barrier semaphores. Data moves between devices by JAX's collectives and lax.ppermute only.
A program may use at most 128 MiB of HBM per device.

v0:
```python
import jax
import jax.numpy as jnp
from jax import lax
from jax.sharding import PartitionSpec as P


def passed_along(x, axis, by):
    length = lax.axis_size(axis)
    pairs = [(i, i + by) for i in range(length) if 0 <= i + by < length]
    return lax.ppermute(x, axis, pairs)


def shifted(x, axis, by):
    length = lax.axis_size(axis)
    return lax.ppermute(x, axis, [(i, (i + by) % length) for i in range(length)])


def partner(x, axis, distance):
    return lax.ppermute(x, axis, [(i, i ^ 1 << distance) for i in range(lax.axis_size(axis))])


def lat_move(field, offset):
    return passed_along(field, "lat", offset)


def lon_move(field, offset):
    return shifted(field, "lon", offset)


def mirror_row(edge_row):
    moved = edge_row
    for bit_number in range(lax.axis_size("lon").bit_length() - 1):
        moved = partner(moved, "lon", bit_number)
    return moved[:, ::-1]


def pad_field(field, is_top, folding):
    south = lat_move(field[-1:], 1)
    north = lat_move(field[:1], -1)
    if folding:
        north = jnp.where(is_top, mirror_row(field[-1:]), north)
    padded = jnp.concatenate([south, field, north], 0)
    west = lon_move(padded[:, -1:], 1)
    east = lon_move(padded[:, :1], -1)
    return jnp.concatenate([west, padded, east], 1)


def silu_slope(value):
    sigma = jax.nn.sigmoid(value)
    return sigma * (1.0 + value * (1.0 - sigma))


def convolve(padded, weights, row_count, col_count):
    total = jnp.zeros((row_count * col_count, weights.shape[2]), jnp.float32)
    for tap_index in range(9):
        row_off, col_off = divmod(tap_index, 3)
        window = padded[row_off : row_off + row_count, col_off : col_off + col_count].reshape(
            row_count * col_count, -1
        )
        total = total + jnp.dot(window, weights[tap_index], preferred_element_type=jnp.float32)
    return total


def kernel_grads(padded, delta, row_count, col_count):
    result = []
    for tap_index in range(9):
        row_off, col_off = divmod(tap_index, 3)
        window = padded[row_off : row_off + row_count, col_off : col_off + col_count].reshape(
            row_count * col_count, -1
        )
        result.append(jnp.einsum("nc,nd->cd", window, delta, preferred_element_type=jnp.float32))
    return jnp.stack(result)


def transpose_conv(delta_pad, weights, is_top, row_count, col_count):
    dims = (((1,), (1,)), ((), ()))
    north = delta_pad[-1:]
    plain = jnp.concatenate([delta_pad[:-1], jnp.where(is_top, jnp.zeros_like(north), north)], 0)
    total = jnp.zeros((row_count * col_count, weights.shape[1]), jnp.float32)
    for tap_index in range(9):
        row_off, col_off = divmod(tap_index, 3)
        window = plain[
            2 - row_off : 2 - row_off + row_count, 2 - col_off : 2 - col_off + col_count
        ].reshape(row_count * col_count, -1)
        total = total + lax.dot_general(
            window, weights[tap_index], dims, preferred_element_type=jnp.float32
        )
    total = total.reshape(row_count, col_count, -1)
    seam_term = jnp.zeros((col_count, weights.shape[1]), jnp.float32)
    for col_off in range(3):
        seam_term = seam_term + lax.dot_general(
            north[0, col_off : col_off + col_count],
            weights[6 + col_off],
            dims,
            preferred_element_type=jnp.float32,
        )
    seam_term = jnp.where(is_top, seam_term, jnp.zeros_like(seam_term))
    return total.at[row_count - 1].add(seam_term)


def body(
    atmos_state,
    atmos_weights,
    flux_project,
    source_row,
    source_col,
    intersection_weight,
    ocean_state,
    flux_inject,
    ocean_mask,
    ocean_weights,
    out_cotangent,
):
    row_count, col_count, chans = atmos_state.shape
    flux_chans = flux_project.shape[1]
    cells = row_count * col_count
    dims = (((1,), (1,)), ((), ()))
    lat_here = lax.axis_index("lat")
    lon_here = lax.axis_index("lon")
    lon_count = lax.axis_size("lon")
    is_top = lat_here == lax.axis_size("lat") - 1
    land = ocean_mask.astype(jnp.float32)[..., None]
    atmos_padded = pad_field(atmos_state, is_top, False)
    atmos_pre = convolve(atmos_padded, atmos_weights, row_count, col_count)
    atmos_act = jax.nn.silu(atmos_pre).astype(jnp.bfloat16)
    flux = jnp.dot(atmos_act, flux_project, preferred_element_type=jnp.float32).astype(jnp.bfloat16)
    flux_flat = flux.reshape(row_count, col_count * flux_chans)
    band = jnp.stack([lon_move(flux_flat, 1), flux_flat, lon_move(flux_flat, -1)])
    neighbourhood = jnp.stack([lat_move(band, 1), band, lat_move(band, -1)]).reshape(
        9 * cells, flux_chans
    )
    tile_dr = source_row // row_count - lat_here
    tile_dc = jnp.remainder(source_col // col_count - lon_here + 1, lon_count) - 1
    slots = (
        ((tile_dr + 1) * 3 + tile_dc + 1) * cells
        + jnp.remainder(source_row, row_count) * col_count
        + jnp.remainder(source_col, col_count)
    )
    picked = jnp.take(neighbourhood, slots, axis=0).astype(jnp.float32)
    remapped = (
        jnp.sum(intersection_weight[..., None] * picked, axis=2)
        .astype(jnp.bfloat16)
        .reshape(cells, flux_chans)
    )
    injected = jnp.dot(remapped, flux_inject, preferred_element_type=jnp.float32).reshape(
        row_count, col_count, chans
    )
    mixed = (land * (ocean_state.astype(jnp.float32) + injected)).astype(jnp.bfloat16)
    ocean_padded = pad_field(mixed, is_top, True)
    ocean_pre = convolve(ocean_padded, ocean_weights, row_count, col_count).reshape(
        row_count, col_count, chans
    )
    ocean_out = (land * jax.nn.silu(ocean_pre)).astype(jnp.bfloat16)
    ocean_delta = (out_cotangent.astype(jnp.float32) * land * silu_slope(ocean_pre)).astype(
        jnp.bfloat16
    )
    grad_ocean = kernel_grads(ocean_padded, ocean_delta.reshape(cells, chans), row_count, col_count)
    delta_padded = pad_field(ocean_delta, is_top, True)
    ocean_back = transpose_conv(delta_padded, ocean_weights, is_top, row_count, col_count)
    mixed_grad = (land * ocean_back).astype(jnp.bfloat16).reshape(cells, chans)
    grad_inject = jnp.einsum("nf,nc->fc", remapped, mixed_grad, preferred_element_type=jnp.float32)
    remap_grad = lax.dot_general(
        mixed_grad, flux_inject, dims, preferred_element_type=jnp.float32
    ).astype(jnp.bfloat16)
    remap_grad = remap_grad.reshape(row_count, col_count, flux_chans)
    contrib_all = intersection_weight[..., None] * remap_grad.astype(jnp.float32)[:, :, None, :]
    credit = (
        jnp.zeros((9 * cells, flux_chans), jnp.float32)
        .at[slots.reshape(-1)]
        .add(contrib_all.reshape(-1, flux_chans))
    )
    credit = credit.astype(jnp.bfloat16).reshape(3, 3, row_count, col_count * flux_chans)
    routed = jnp.stack([lat_move(credit[2], 1), credit[1], lat_move(credit[0], -1)])
    from_east = lon_move(routed[:, 0], -1)
    from_west = lon_move(routed[:, 2], 1)
    flux_sum = (
        jnp.sum(routed[:, 1].astype(jnp.float32), 0)
        + jnp.sum(from_east.astype(jnp.float32), 0)
        + jnp.sum(from_west.astype(jnp.float32), 0)
    )
    flux_grad = flux_sum.astype(jnp.bfloat16).reshape(cells, flux_chans)
    grad_project = jnp.einsum("nc,nf->cf", atmos_act, flux_grad, preferred_element_type=jnp.float32)
    act_grad = lax.dot_general(flux_grad, flux_project, dims, preferred_element_type=jnp.float32)
    atmos_delta = (act_grad * silu_slope(atmos_pre)).astype(jnp.bfloat16)
    grad_atmos = kernel_grads(atmos_padded, atmos_delta, row_count, col_count)
    grad_atmos, grad_ocean, grad_project, grad_inject = lax.psum(
        (grad_atmos, grad_ocean, grad_project, grad_inject), ("lon", "lat")
    )
    return (ocean_out, grad_atmos, grad_ocean, grad_project, grad_inject)


def solution(mesh):
    return jax.shard_map(
        body,
        mesh=mesh,
        in_specs=(
            P("lat", "lon", None),
            P(),
            P(),
            P("lat", "lon", None),
            P("lat", "lon", None),
            P("lat", "lon", None),
            P("lat", "lon", None),
            P(),
            P("lat", "lon"),
            P(),
            P("lat", "lon", None),
        ),
        out_specs=(P("lat", "lon", None), P(), P(), P(), P()),
        check_vma=False,
    )
```

profile of v0, /device:TPU:1, one launch (start us, length us, event | category | flops | bytes accessed | tf_op | source)
XLA Modules:
  0.0 516.5 jit_solution(17819121093324775576)
XLA Ops:
  8.0 4.5 collective-permute-start
  23.1 3.6 collective-permute-start.3
  27.9 3.8 pad_maximum_fusion.11
  40.4 5.2 %collective-permute-start.5 = (bf16[32,4096]{1,0:T(8,128)(2,1)S(1)}, bf16[32,4096]{1,0:T(8,128)(2,1)S(1)}, u32[]{:S(2)}, u32[]{:S(2)}) collective-permute-start(bf16[32,4096]{1,0:T(8,128)(2,1)S(1)} %reshape.233), channel_id=1, source_target_pairs={{0,112},{16,0},{32,16},{48,32},{64,48},{80,64},{96,80},{112,96},{1... | collective-permute-start | bytes 786440 | tf_op jit(solution)/shard_map/ppermute | solution.py:15
  46.1 5.6 %collective-permute-done.5 = bf16[32,4096]{1,0:T(8,128)(2,1)S(1)} collective-permute-done((bf16[32,4096]{1,0:T(8,128)(2,1)S(1)}, bf16[32,4096]{1,0:T(8,128)(2,1)S(1)}, u32[]{:S(2)}, u32[]{:S(2)}) %collective-permute-start.5) | collective-permute-done | bytes 262176 | tf_op jit(solution)/shard_map/ppermute | solution.py:15
  51.7 6.7 %collective-permute-done.4 = bf16[32,4096]{1,0:T(8,128)(2,1)S(1)} collective-permute-done((bf16[32,4096]{1,0:T(8,128)(2,1)S(1)}, bf16[32,4096]{1,0:T(8,128)(2,1)S(1)}, u32[]{:S(2)}, u32[]{:S(2)}) %collective-permute-start.4) | collective-permute-done | bytes 262176 | tf_op jit(solution)/shard_map/ppermute | solution.py:15
  61.7 3.7 collective-permute-start.6
  76.9 6.2 %reshape.234 = bf16[18432,64]{1,0:T(8,128)(2,1)} reshape(bf16[3,3,32,4096]{3,2,1,0:T(8,128)(2,1)S(1)} %pad_maximum_fusion) | data formatting | bytes 4718592 | tf_op jit(solution)/shard_map/reshape | solution.py:129
  83.1 31.3 %gather_fusion = bf16[8192,64]{1,0:T(8,128)(2,1)} fusion(bf16[18432,64]{1,0:T(8,128)(2,1)} %reshape.234, s32[8192]{0:T(1024)S(1)} %broadcast_clamp_fusion), kind=kCustom, calls=%fused_computation | custom fusion | bytes 2129920 | tf_op jit(solution)/shard_map/jit(_take)/gather | solution.py:139
  114.4 6.9 %multiply_reduce_fusion = bf16[32,64,64]{2,1,0:T(8,128)(2,1)S(1)} fusion(bf16[32,64,4,64]{3,2,1,0:T(4,128)(2,1)} %bitcast.318, f32[32,64,4]{2,1,0:T(8,128)S(1)} %copy-done.20, pred[32,64,4]{2,1,0:T(8,128)(4,1)S(1)} %copy-done.36), kind=kLoop, calls=%fused_computation.5 | loop fusion | flops 1966080 | bytes 1351680 | tf_op jit(solution)/shard_map/reduce_sum | solution.py:141
  132.8 6.1 %collective-permute-start.8 = (bf16[1,64,256]{2,1,0:T(8,128)(2,1)S(1)}, bf16[1,64,256]{2,1,0:T(8,128)(2,1)S(1)}, u32[]{:S(2)}, u32[]{:S(2)}) collective-permute-start(bf16[1,64,256]{2,1,0:T(8,128)(2,1)S(1)} %get-tuple-element.67), channel_id=1, source_target_pairs={{0,1},{1,2},{2,3},{3,4},{4,5},{5,6},{6,7},{7,8},{8,9},{9,10},{10,1... | collective-permute-start | bytes 98312 | tf_op jit(solution)/shard_map/ppermute | solution.py:10
  139.9 4.5 collective-permute-start.14
  145.5 5.5 %collective-permute-done.13 = bf16[34,1,256]{2,1,0:T(2,128)(2,1)S(1)} collective-permute-done((bf16[34,1,256]{2,1,0:T(2,128)(2,1)S(1)}, bf16[34,1,256]{2,1,0:T(2,128)(2,1)S(1)}, u32[]{:S(2)}, u32[]{:S(2)}) %collective-permute-start.13) | collective-permute-done | bytes 17440 | tf_op jit(solution)/shard_map/ppermute | solution.py:15
  159.7 5.6 %collective-permute-start.15 = (bf16[1,64,256]{2,1,0:T(8,128)(2,1)S(1)}, bf16[1,64,256]{2,1,0:T(8,128)(2,1)S(1)}, u32[]{:S(2)}, u32[]{:S(2)}) collective-permute-start(bf16[1,64,256]{2,1,0:T(8,128)(2,1)S(1)} %get-tuple-element.63), channel_id=1, source_target_pairs={{0,1},{1,2},{2,3},{3,4},{4,5},{5,6},{6,7},{7,8},{8,9},{9,10},{10,1... | collective-permute-start | bytes 98312 | tf_op jit(solution)/shard_map/ppermute | solution.py:10
  174.7 3.3 collective-permute-done.18
  184.4 4.7 collective-permute-done.20
  203.7 4.0 mul.113
  207.7 52.9 %scatter_custom_fusion = f32[18432,64]{1,0:T(8,128)} fusion(s32[8192]{0:T(1024)} %bitcast.345, f32[]{:T(128)} %constant.131.clone.1, f32[8192,64]{1,0:T(8,128)} %bitcast.301, f32[8192]{0:T(1024)S(1)} %mul.106), kind=kCustom, calls=%fused_computation.2 | custom fusion | flops 1048576 | bytes 8946176 | tf_op jit(solution)/shard_map/scatter-add | solution.py:170
  260.6 4.3 convert_element_type.85
  275.6 6.5 %collective-permute-start.22 = (bf16[3,32,4096]{2,1,0:T(8,128)(2,1)}, bf16[3,32,4096]{2,1,0:T(8,128)(2,1)}, u32[]{:S(2)}, u32[]{:S(2)}) collective-permute-start(bf16[3,32,4096]{2,1,0:T(8,128)(2,1)} %squeeze.109), channel_id=1, source_target_pairs={{0,1},{1,2},{2,3},{3,4},{4,5},{5,6},{6,7},{7,8},{8,9},{9,10},{10,1... | collective-permute-start | bytes 2359304 | tf_op jit(solution)/shard_map/ppermute | solution.py:10
  299.5 20.1 %collective-permute-done.24 = bf16[3,32,4096]{2,1,0:T(8,128)(2,1)S(1)} collective-permute-done((bf16[3,32,4096]{2,1,0:T(8,128)(2,1)S(1)}, bf16[3,32,4096]{2,1,0:T(8,128)(2,1)S(1)}, u32[]{:S(2)}, u32[]{:S(2)}) %collective-permute-start.24) | collective-permute-done | bytes 786464 | tf_op jit(solution)/shard_map/ppermute | solution.py:15
  319.8 12.5 %collective-permute-done.25 = bf16[3,32,4096]{2,1,0:T(8,128)(2,1)S(1)} collective-permute-done((bf16[3,32,4096]{2,1,0:T(8,128)(2,1)S(1)}, bf16[3,32,4096]{2,1,0:T(8,128)(2,1)S(1)}, u32[]{:S(2)}, u32[]{:S(2)}) %collective-permute-start.25) | collective-permute-done | bytes 786464 | tf_op jit(solution)/shard_map/ppermute | solution.py:15
  344.1 159.4 %all-reduce.3.cloned.1.call-done = (f32[9,256,256]{2,1,0:T(8,128)}, f32[9,256,256]{2,1,0:T(8,128)}, f32[256,64]{0,1:T(8,128)}, f32[64,256]{1,0:T(8,128)}) async-done(((f32[9,256,256]{2,1,0:T(8,128)}, f32[9,256,256]{2,1,0:T(8,128)}, f32[256,64]{0,1:T(8,128)}, f32[64,256]{1,0:T(8,128)}), (f32[9,256,256]{2,1,0:T(8,128)}, f32[9,256,256]{2,1,0:T(8,128)}, f32[256,64]{0,1:T(8,128)}, ...) | async-done | bytes 4849680 | tf_op jit(solution)/shard_map/psum | solution.py:186
  503.5 3.4 copy.67
  (242 shorter events, 131.0 us)
Async XLA Ops:
  7.2 496.3 %all-reduce.3.cloned.1.call-start = ((), (), s32[]{:S(2)}) async-start(), calls=%async_computation | async-start | bytes 9699328 | tf_op jit(solution)/shard_map/psum | solution.py:186
  8.0 6.4 %collective-permute-start = (bf16[1,64,256]{2,1,0:T(8,128)(2,1)S(1)}, bf16[1,64,256]{2,1,0:T(8,128)(2,1)S(1)}, u32[]{:S(2)}, u32[]{:S(2)}) collective-permute-start(bf16[1,64,256]{2,1,0:T(8,128)(2,1)S(1)} %get-tuple-element.72), channel_id=1, source_target_pairs={{0,1},{1,2},{2,3},{3,4},{4,5},{5,6},{6,7},{7,8},{8,9},{9,10},{10,1... | collective-permute-start | bytes 98312 | tf_op jit(solution)/shard_map/ppermute | solution.py:10
  12.5 5.2 %collective-permute-start.1 = (bf16[1,64,256]{2,1,0:T(8,128)(2,1)S(1)}, bf16[1,64,256]{2,1,0:T(8,128)(2,1)S(1)}, u32[]{:S(2)}, u32[]{:S(2)}) collective-permute-start(bf16[1,64,256]{2,1,0:T(8,128)(2,1)S(1)} %get-tuple-element.71), channel_id=1, source_target_pairs={{1,0},{2,1},{3,2},{4,3},{5,4},{6,5},{7,6},{8,7},{9,8},{10,9},{11,1... | collective-permute-start | bytes 98312 | tf_op jit(solution)/shard_map/ppermute | solution.py:10
  20.1 7.8 %collective-permute-start.2 = (bf16[34,1,256]{2,1,0:T(2,128)(2,1)S(1)}, bf16[34,1,256]{2,1,0:T(2,128)(2,1)S(1)}, u32[]{:S(2)}, u32[]{:S(2)}) collective-permute-start(bf16[34,1,256]{2,1,0:T(2,128)(2,1)S(1)} %get-tuple-element.60), channel_id=1, source_target_pairs={{0,16},{16,32},{32,48},{48,64},{64,80},{80,96},{96,112},{112,0},{1... | collective-permute-start | bytes 52232 | tf_op jit(solution)/shard_map/ppermute | solution.py:15
  23.1 4.8 collective-permute-start.3
  40.4 11.3 %collective-permute-start.5 = (bf16[32,4096]{1,0:T(8,128)(2,1)S(1)}, bf16[32,4096]{1,0:T(8,128)(2,1)S(1)}, u32[]{:S(2)}, u32[]{:S(2)}) collective-permute-start(bf16[32,4096]{1,0:T(8,128)(2,1)S(1)} %reshape.233), channel_id=1, source_target_pairs={{0,112},{16,0},{32,16},{48,32},{64,48},{80,64},{96,80},{112,96},{1... | collective-permute-start | bytes 786440 | tf_op jit(solution)/shard_map/ppermute | solution.py:15
  45.6 12.8 %collective-permute-start.4 = (bf16[32,4096]{1,0:T(8,128)(2,1)S(1)}, bf16[32,4096]{1,0:T(8,128)(2,1)S(1)}, u32[]{:S(2)}, u32[]{:S(2)}) collective-permute-start(bf16[32,4096]{1,0:T(8,128)(2,1)S(1)} %reshape.233), channel_id=1, source_target_pairs={{0,16},{16,32},{32,48},{48,64},{64,80},{80,96},{96,112},{112,0},{1... | collective-permute-start | bytes 786440 | tf_op jit(solution)/shard_map/ppermute | solution.py:15
  59.4 13.6 %collective-permute-start.7 = (bf16[3,32,4096]{2,1,0:T(8,128)(2,1)S(1)}, bf16[3,32,4096]{2,1,0:T(8,128)(2,1)S(1)}, u32[]{:S(2)}, u32[]{:S(2)}) collective-permute-start(bf16[3,32,4096]{2,1,0:T(8,128)(2,1)S(1)} %get-tuple-element.74), channel_id=1, source_target_pairs={{1,0},{2,1},{3,2},{4,3},{5,4},{6,5},{7,6},{8,7},{9,8},{10,9},{11,1... | collective-permute-start | bytes 2359304 | tf_op jit(solution)/shard_map/ppermute | solution.py:10
  61.7 12.5 %collective-permute-start.6 = (bf16[3,32,4096]{2,1,0:T(8,128)(2,1)S(1)}, bf16[3,32,4096]{2,1,0:T(8,128)(2,1)S(1)}, u32[]{:S(2)}, u32[]{:S(2)}) collective-permute-start(bf16[3,32,4096]{2,1,0:T(8,128)(2,1)S(1)} %get-tuple-element.74), channel_id=1, source_target_pairs={{0,1},{1,2},{2,3},{3,4},{4,5},{5,6},{6,7},{7,8},{8,9},{9,10},{10,1... | collective-permute-start | bytes 2359304 | tf_op jit(solution)/shard_map/ppermute | solution.py:10
  128.2 10.8 %collective-permute-start.12 = (bf16[1,64,256]{2,1,0:T(8,128)(2,1)S(1)}, bf16[1,64,256]{2,1,0:T(8,128)(2,1)S(1)}, u32[]{:S(2)}, u32[]{:S(2)}) collective-permute-start(bf16[1,64,256]{2,1,0:T(8,128)(2,1)S(1)} %get-tuple-element.66), channel_id=1, source_target_pairs={{1,0},{2,1},{3,2},{4,3},{5,4},{6,5},{7,6},{8,7},{9,8},{10,9},{11,1... | collective-permute-start | bytes 98312 | tf_op jit(solution)/shard_map/ppermute | solution.py:10
  130.1 8.8 %collective-permute-start.11 = (bf16[1,64,256]{2,1,0:T(8,128)(2,1)S(1)}, bf16[1,64,256]{2,1,0:T(8,128)(2,1)S(1)}, u32[]{:S(2)}, u32[]{:S(2)}) collective-permute-start(bf16[1,64,256]{2,1,0:T(8,128)(2,1)S(1)} %collective-permute-done.10), channel_id=1, source_target_pairs={{0,64},{16,80},{32,96},{48,112},{64,0},{80,16},{96,32},{112,48},{1... | collective-permute-start | bytes 98312 | tf_op jit(solution)/shard_map/ppermute | solution.py:19
  132.8 7.1 %collective-permute-start.8 = (bf16[1,64,256]{2,1,0:T(8,128)(2,1)S(1)}, bf16[1,64,256]{2,1,0:T(8,128)(2,1)S(1)}, u32[]{:S(2)}, u32[]{:S(2)}) collective-permute-start(bf16[1,64,256]{2,1,0:T(8,128)(2,1)S(1)} %get-tuple-element.67), channel_id=1, source_target_pairs={{0,1},{1,2},{2,3},{3,4},{4,5},{5,6},{6,7},{7,8},{8,9},{9,10},{10,1... | collective-permute-start | bytes 98312 | tf_op jit(solution)/shard_map/ppermute | solution.py:10
  139.9 5.5 %collective-permute-start.14 = (bf16[34,1,256]{2,1,0:T(2,128)(2,1)S(1)}, bf16[34,1,256]{2,1,0:T(2,128)(2,1)S(1)}, u32[]{:S(2)}, u32[]{:S(2)}) collective-permute-start(bf16[34,1,256]{2,1,0:T(2,128)(2,1)S(1)} %get-tuple-element.55), channel_id=1, source_target_pairs={{0,112},{16,0},{32,16},{48,32},{64,48},{80,64},{96,80},{112,96},{1... | collective-permute-start | bytes 52232 | tf_op jit(solution)/shard_map/ppermute | solution.py:15
  144.4 6.6 %collective-permute-start.13 = (bf16[34,1,256]{2,1,0:T(2,128)(2,1)S(1)}, bf16[34,1,256]{2,1,0:T(2,128)(2,1)S(1)}, u32[]{:S(2)}, u32[]{:S(2)}) collective-permute-start(bf16[34,1,256]{2,1,0:T(2,128)(2,1)S(1)} %get-tuple-element.56), channel_id=1, source_target_pairs={{0,16},{16,32},{32,48},{48,64},{64,80},{80,96},{96,112},{112,0},{1... | collective-permute-start | bytes 52232 | tf_op jit(solution)/shard_map/ppermute | solution.py:15
  159.7 11.1 %collective-permute-start.16 = (bf16[1,64,256]{2,1,0:T(8,128)(2,1)S(1)}, bf16[1,64,256]{2,1,0:T(8,128)(2,1)S(1)}, u32[]{:S(2)}, u32[]{:S(2)}) collective-permute-start(bf16[1,64,256]{2,1,0:T(8,128)(2,1)S(1)} %get-tuple-element.63), channel_id=1, source_target_pairs={{0,16},{16,0},{32,48},{48,32},{64,80},{80,64},{96,112},{112,96},{1... | collective-permute-start | bytes 98312 | tf_op jit(solution)/shard_map/ppermute | solution.py:19
  159.7 14.0 %collective-permute-start.15 = (bf16[1,64,256]{2,1,0:T(8,128)(2,1)S(1)}, bf16[1,64,256]{2,1,0:T(8,128)(2,1)S(1)}, u32[]{:S(2)}, u32[]{:S(2)}) collective-permute-start(bf16[1,64,256]{2,1,0:T(8,128)(2,1)S(1)} %get-tuple-element.63), channel_id=1, source_target_pairs={{0,1},{1,2},{2,3},{3,4},{4,5},{5,6},{6,7},{7,8},{8,9},{9,10},{10,1... | collective-permute-start | bytes 98312 | tf_op jit(solution)/shard_map/ppermute | solution.py:10
  166.5 12.3 %collective-permute-start.19 = (bf16[1,64,256]{2,1,0:T(8,128)(2,1)}, bf16[1,64,256]{2,1,0:T(8,128)(2,1)}, u32[]{:S(2)}, u32[]{:S(2)}) collective-permute-start(bf16[1,64,256]{2,1,0:T(8,128)(2,1)} %get-tuple-element.62), channel_id=1, source_target_pairs={{1,0},{2,1},{3,2},{4,3},{5,4},{6,5},{7,6},{8,7},{9,8},{10,9},{11,1... | collective-permute-start | bytes 98312 | tf_op jit(solution)/shard_map/ppermute | solution.py:10
  173.6 4.4 collective-permute-start.18
  179.6 4.8 collective-permute-start.21
  182.3 6.8 %collective-permute-start.20 = (bf16[34,1,256]{2,1,0:T(2,128)(2,1)S(1)}, bf16[34,1,256]{2,1,0:T(2,128)(2,1)S(1)}, u32[]{:S(2)}, u32[]{:S(2)}) collective-permute-start(bf16[34,1,256]{2,1,0:T(2,128)(2,1)S(1)} %get-tuple-element.52), channel_id=1, source_target_pairs={{0,16},{16,32},{32,48},{48,64},{64,80},{80,96},{96,112},{112,0},{1... | collective-permute-start | bytes 52232 | tf_op jit(solution)/shard_map/ppermute | solution.py:15
  273.5 16.6 %collective-permute-start.23 = (bf16[3,32,4096]{2,1,0:T(8,128)(2,1)}, bf16[3,32,4096]{2,1,0:T(8,128)(2,1)}, u32[]{:S(2)}, u32[]{:S(2)}) collective-permute-start(bf16[3,32,4096]{2,1,0:T(8,128)(2,1)} %squeeze.110), channel_id=1, source_target_pairs={{1,0},{2,1},{3,2},{4,3},{5,4},{6,5},{7,6},{8,7},{9,8},{10,9},{11,1... | collective-permute-start | bytes 2359304 | tf_op jit(solution)/shard_map/ppermute | solution.py:10
  275.6 15.7 %collective-permute-start.22 = (bf16[3,32,4096]{2,1,0:T(8,128)(2,1)}, bf16[3,32,4096]{2,1,0:T(8,128)(2,1)}, u32[]{:S(2)}, u32[]{:S(2)}) collective-permute-start(bf16[3,32,4096]{2,1,0:T(8,128)(2,1)} %squeeze.109), channel_id=1, source_target_pairs={{0,1},{1,2},{2,3},{3,4},{4,5},{5,6},{6,7},{7,8},{8,9},{9,10},{10,1... | collective-permute-start | bytes 2359304 | tf_op jit(solution)/shard_map/ppermute | solution.py:10
  293.0 26.6 %collective-permute-start.24 = (bf16[3,32,4096]{2,1,0:T(8,128)(2,1)S(1)}, bf16[3,32,4096]{2,1,0:T(8,128)(2,1)S(1)}, u32[]{:S(2)}, u32[]{:S(2)}) collective-permute-start(bf16[3,32,4096]{2,1,0:T(8,128)(2,1)S(1)} %get-tuple-element.26), channel_id=1, source_target_pairs={{0,112},{16,0},{32,16},{48,32},{64,48},{80,64},{96,80},{112,96},{1... | collective-permute-start | bytes 2359304 | tf_op jit(solution)/shard_map/ppermute | solution.py:15
  293.1 39.1 %collective-permute-start.25 = (bf16[3,32,4096]{2,1,0:T(8,128)(2,1)S(1)}, bf16[3,32,4096]{2,1,0:T(8,128)(2,1)S(1)}, u32[]{:S(2)}, u32[]{:S(2)}) collective-permute-start(bf16[3,32,4096]{2,1,0:T(8,128)(2,1)S(1)} %get-tuple-element.27), channel_id=1, source_target_pairs={{0,16},{16,32},{32,48},{48,64},{64,80},{80,96},{96,112},{112,0},{1... | collective-permute-start | bytes 2359304 | tf_op jit(solution)/shard_map/ppermute | solution.py:15
  (48 other events, 359.9 us)
Sparse Core Ops, SparseCore 0:
  344.2 159.2 all-reduce.2
where the time goes:
time: 524 us; the launch traced here: 517 us
  waiting for transfers between devices  231 us (44%)
  other arithmetic  85.4 us (16%)
  local copies, waits for them, and re-layouts  84.4 us (16%)
  starting transfers between devices  63.3 us (12%)
  matrix products  36.9 us (7%)
  between operations  15.2 us (3%)
    psum x1, waiting for transfers between devices, body(): lax.psum((grad_atmos, grad_ocean, grad_project, grad_inject), ('lon', 'la...  159 us
    ppermute x10, waiting for transfers between devices, shifted(): lax.ppermute(x, axis, [(i, (i + by) % length) for i in range(length)])  55.8 us
    scatter-add x1, other arithmetic, body(): credit = jnp.zeros((9 * cells, flux_chans), jnp.float32).at[slots.reshape...  52.9 us
    ppermute x10, starting transfers between devices, passed_along(): return lax.ppermute(x, axis, pairs)  36.5 us
    gather x1, local copies, waits for them, and re-layouts, body(): picked = jnp.take(neighbourhood, slots, axis=0).astype(jnp.float32)  31.3 us
    ppermute x10, starting transfers between devices, shifted(): lax.ppermute(x, axis, [(i, (i + by) % length) for i in range(length)])  23.2 us
    unnamed x97, local copies, waits for them, and re-layouts  18.9 us
    dot_general x18, matrix products, kernel_grads(): jnp.einsum('nc,nd->cd', window, delta, preferred_element_type=jnp.float32)  15.1 us
  transfers between devices with their start and end apart: 27, of which 18 were waited for; matrix products, arithmetic and copies ran while one was open for 6% of the time, Pallas kernels for 0%

commit v1 on v0

--- a/solution.py
+++ b/solution.py
@@ -184,7 +184,7 @@
     atmos_delta = (act_grad * silu_slope(atmos_pre)).astype(jnp.bfloat16)
     grad_atmos = kernel_grads(atmos_padded, atmos_delta, row_count, col_count)
     grad_atmos, grad_ocean, grad_project, grad_inject = lax.psum(
-        (grad_atmos, grad_ocean, grad_project, grad_inject), ("lon", "lat")
+        lax.psum((grad_atmos, grad_ocean, grad_project, grad_inject), "lon"), "lat"
     )
     return (ocean_out, grad_atmos, grad_ocean, grad_project, grad_inject)
 

time: 524 us -> 705 us (1.35)
  waiting for transfers between devices: 231 us -> 424 us
  local copies, waits for them, and re-layouts: 84.4 us -> 75 us
    psum x1 -> x2, waiting for transfers between devices: 159 us -> 348 us  [the longest x1 215 us: body(): lax.psum((grad_atmos, grad_ocean, grad_project, grad_inject), 'lon')]
    unnamed x97 -> x101, local copies, waits for them, and re-layouts: 18.9 us -> 16.1 us
  transfers between devices with their start and end apart: 27 -> 28, of which waited for: 18 -> 19; matrix products, arithmetic and copies ran while one was open for 6% -> 4% of each run, Pallas kernels for 0% -> 0%
where the time goes in v1:
time: 705 us; the launch traced here: 697 us
  waiting for transfers between devices  424 us (60%)
  other arithmetic  82.3 us (12%)
  local copies, waits for them, and re-layouts  75 us (11%)
  starting transfers between devices  63.4 us (9%)
  matrix products  37 us (5%)
  between operations  15.3 us (2%)
    psum x1, waiting for transfers between devices, body(): lax.psum((grad_atmos, grad_ocean, grad_project, grad_inject), 'lon')  215 us
    psum x1, waiting for transfers between devices, body(): lax.psum(lax.psum((grad_atmos, grad_ocean, grad_project, grad_inject), 'l...  133 us
    ppermute x10, waiting for transfers between devices, shifted(): lax.ppermute(x, axis, [(i, (i + by) % length) for i in range(length)])  55.7 us
    scatter-add x1, other arithmetic, body(): credit = jnp.zeros((9 * cells, flux_chans), jnp.float32).at[slots.reshape...  52.9 us
    ppermute x10, starting transfers between devices, passed_along(): return lax.ppermute(x, axis, pairs)  36.5 us
    gather x1, local copies, waits for them, and re-layouts, body(): picked = jnp.take(neighbourhood, slots, axis=0).astype(jnp.float32)  24.9 us
    ppermute x10, starting transfers between devices, shifted(): lax.ppermute(x, axis, [(i, (i + by) % length) for i in range(length)])  23.2 us
    unnamed x101, local copies, waits for them, and re-layouts  16.1 us
  transfers between devices with their start and end apart: 28, of which 19 were waited for; matrix products, arithmetic and copies ran while one was open for 4% of the time, Pallas kernels for 0%

profile of v1, /device:TPU:1, one launch (start us, length us, event | category | flops | bytes accessed | tf_op | source)
XLA Modules:
  0.0 697.4 jit_solution(12341995931313144478)
XLA Ops:
  8.0 4.5 collective-permute-start
  23.1 3.6 collective-permute-start.3
  27.9 3.8 pad_maximum_fusion.11
  40.5 5.2 collective-permute-start.5
  46.2 5.6 collective-permute-done.5
  51.8 6.7 collective-permute-done.4
  62.0 3.7 collective-permute-start.6
  68.8 4.7 collective-permute-done.7
  76.7 6.1 reshape.234
  82.8 24.9 %gather_fusion = bf16[8192,64]{1,0:T(8,128)(2,1)S(1)} fusion(bf16[18432,64]{1,0:T(8,128)(2,1)} %reshape.234, s32[8192]{0:T(1024)S(1)} %broadcast_clamp_fusion), kind=kCustom, calls=%fused_computation | custom fusion | bytes 2129920 | tf_op jit(solution)/shard_map/jit(_take)/gather | solution.py:139
  107.7 5.9 multiply_reduce_fusion
  125.6 6.1 collective-permute-start.8
  132.8 4.5 collective-permute-start.14
  138.3 5.5 collective-permute-done.13
  152.5 5.6 collective-permute-start.15
  176.5 4.7 collective-permute-done.20
  195.7 4.1 mul.113
  199.8 52.9 %scatter_custom_fusion = f32[18432,64]{1,0:T(8,128)} fusion(s32[8192]{0:T(1024)} %bitcast.344, f32[]{:T(128)} %constant.131.clone.1, f32[8192,64]{1,0:T(8,128)} %bitcast.301, f32[8192]{0:T(1024)S(1)} %copy-done.38), kind=kCustom, calls=%fused_computation.2 | custom fusion | flops 1048576 | bytes 8946176 | tf_op jit(solution)/shard_map/scatter-add | solution.py:170
  252.7 4.3 convert_element_type.85
  267.7 6.5 collective-permute-start.22
  291.6 20.1 %collective-permute-done.24 = bf16[3,32,4096]{2,1,0:T(8,128)(2,1)S(1)} collective-permute-done((bf16[3,32,4096]{2,1,0:T(8,128)(2,1)S(1)}, bf16[3,32,4096]{2,1,0:T(8,128)(2,1)S(1)}, u32[]{:S(2)}, u32[]{:S(2)}) %collective-permute-start.24) | collective-permute-done | bytes 786464 | tf_op jit(solution)/shard_map/ppermute | solution.py:15
  311.9 12.5 %collective-permute-done.25 = bf16[3,32,4096]{2,1,0:T(8,128)(2,1)S(1)} collective-permute-done((bf16[3,32,4096]{2,1,0:T(8,128)(2,1)S(1)}, bf16[3,32,4096]{2,1,0:T(8,128)(2,1)S(1)}, u32[]{:S(2)}, u32[]{:S(2)}) %collective-permute-start.25) | collective-permute-done | bytes 786464 | tf_op jit(solution)/shard_map/ppermute | solution.py:15
  336.2 214.6 %all-reduce.7.cloned.1.call-done = (f32[9,256,256]{2,1,0:T(8,128)}, f32[9,256,256]{2,1,0:T(8,128)}, f32[256,64]{0,1:T(8,128)}, f32[64,256]{1,0:T(8,128)}) async-done(((f32[9,256,256]{2,1,0:T(8,128)}, f32[9,256,256]{2,1,0:T(8,128)}, f32[256,64]{0,1:T(8,128)}, f32[64,256]{1,0:T(8,128)}), (f32[9,256,256]{2,1,0:T(8,128)}, f32[9,256,256]{2,1,0:T(8,128)}, f32[256,64]{0,1:T(8,128)}, ...) | async-done | bytes 4849680 | tf_op jit(solution)/shard_map/psum | solution.py:187
  550.8 133.5 %all-reduce.5.cloned.1.call-done = (f32[9,256,256]{2,1,0:T(8,128)}, f32[9,256,256]{2,1,0:T(8,128)}, f32[256,64]{0,1:T(8,128)}, f32[64,256]{1,0:T(8,128)}) async-done(((f32[9,256,256]{2,1,0:T(8,128)}, f32[9,256,256]{2,1,0:T(8,128)}, f32[256,64]{0,1:T(8,128)}, f32[64,256]{1,0:T(8,128)}), (f32[9,256,256]{2,1,0:T(8,128)}, f32[9,256,256]{2,1,0:T(8,128)}, f32[256,64]{0,1:T(8,128)}, ...) | async-done | bytes 4849680 | tf_op jit(solution)/shard_map/psum | solution.py:186
  (249 shorter events, 132.4 us)
Async XLA Ops:
  7.2 543.6 %all-reduce.7.cloned.1.call-start = ((), (), s32[]{:S(2)}) async-start(), calls=%async_computation.1 | async-start | bytes 9699328 | tf_op jit(solution)/shard_map/psum | solution.py:187
  8.0 6.4 collective-permute-start
  12.5 5.2 collective-permute-start.1
  20.1 7.8 %collective-permute-start.2 = (bf16[34,1,256]{2,1,0:T(2,128)(2,1)S(1)}, bf16[34,1,256]{2,1,0:T(2,128)(2,1)S(1)}, u32[]{:S(2)}, u32[]{:S(2)}) collective-permute-start(bf16[34,1,256]{2,1,0:T(2,128)(2,1)S(1)} %get-tuple-element.64), channel_id=1, source_target_pairs={{0,16},{16,32},{32,48},{48,64},{64,80},{80,96},{96,112},{112,0},{1... | collective-permute-start | bytes 52232 | tf_op jit(solution)/shard_map/ppermute | solution.py:15
  23.1 4.8 collective-permute-start.3
  40.5 11.3 %collective-permute-start.5 = (bf16[32,4096]{1,0:T(8,128)(2,1)S(1)}, bf16[32,4096]{1,0:T(8,128)(2,1)S(1)}, u32[]{:S(2)}, u32[]{:S(2)}) collective-permute-start(bf16[32,4096]{1,0:T(8,128)(2,1)S(1)} %reshape.233), channel_id=1, source_target_pairs={{0,112},{16,0},{32,16},{48,32},{64,48},{80,64},{96,80},{112,96},{1... | collective-permute-start | bytes 786440 | tf_op jit(solution)/shard_map/ppermute | solution.py:15
  45.7 12.8 %collective-permute-start.4 = (bf16[32,4096]{1,0:T(8,128)(2,1)S(1)}, bf16[32,4096]{1,0:T(8,128)(2,1)S(1)}, u32[]{:S(2)}, u32[]{:S(2)}) collective-permute-start(bf16[32,4096]{1,0:T(8,128)(2,1)S(1)} %reshape.233), channel_id=1, source_target_pairs={{0,16},{16,32},{32,48},{48,64},{64,80},{80,96},{96,112},{112,0},{1... | collective-permute-start | bytes 786440 | tf_op jit(solution)/shard_map/ppermute | solution.py:15
  59.7 13.8 %collective-permute-start.7 = (bf16[3,32,4096]{2,1,0:T(8,128)(2,1)}, bf16[3,32,4096]{2,1,0:T(8,128)(2,1)S(1)}, u32[]{:S(2)}, u32[]{:S(2)}) collective-permute-start(bf16[3,32,4096]{2,1,0:T(8,128)(2,1)} %get-tuple-element.78), channel_id=1, source_target_pairs={{1,0},{2,1},{3,2},{4,3},{5,4},{6,5},{7,6},{8,7},{9,8},{10,9},{11,1... | collective-permute-start | bytes 2359304 | tf_op jit(solution)/shard_map/ppermute | solution.py:10
  62.0 12.8 %collective-permute-start.6 = (bf16[3,32,4096]{2,1,0:T(8,128)(2,1)}, bf16[3,32,4096]{2,1,0:T(8,128)(2,1)}, u32[]{:S(2)}, u32[]{:S(2)}) collective-permute-start(bf16[3,32,4096]{2,1,0:T(8,128)(2,1)} %get-tuple-element.78), channel_id=1, source_target_pairs={{0,1},{1,2},{2,3},{3,4},{4,5},{5,6},{6,7},{7,8},{8,9},{9,10},{10,1... | collective-permute-start | bytes 2359304 | tf_op jit(solution)/shard_map/ppermute | solution.py:10
  120.4 11.4 %collective-permute-start.12 = (bf16[1,64,256]{2,1,0:T(8,128)(2,1)S(1)}, bf16[1,64,256]{2,1,0:T(8,128)(2,1)S(1)}, u32[]{:S(2)}, u32[]{:S(2)}) collective-permute-start(bf16[1,64,256]{2,1,0:T(8,128)(2,1)S(1)} %get-tuple-element.70), channel_id=1, source_target_pairs={{1,0},{2,1},{3,2},{4,3},{5,4},{6,5},{7,6},{8,7},{9,8},{10,9},{11,1... | collective-permute-start | bytes 98312 | tf_op jit(solution)/shard_map/ppermute | solution.py:10
  122.3 9.4 %collective-permute-start.11 = (bf16[1,64,256]{2,1,0:T(8,128)(2,1)S(1)}, bf16[1,64,256]{2,1,0:T(8,128)(2,1)S(1)}, u32[]{:S(2)}, u32[]{:S(2)}) collective-permute-start(bf16[1,64,256]{2,1,0:T(8,128)(2,1)S(1)} %collective-permute-done.10), channel_id=1, source_target_pairs={{0,64},{16,80},{32,96},{48,112},{64,0},{80,16},{96,32},{112,48},{1... | collective-permute-start | bytes 98312 | tf_op jit(solution)/shard_map/ppermute | solution.py:19
  125.6 7.1 %collective-permute-start.8 = (bf16[1,64,256]{2,1,0:T(8,128)(2,1)S(1)}, bf16[1,64,256]{2,1,0:T(8,128)(2,1)S(1)}, u32[]{:S(2)}, u32[]{:S(2)}) collective-permute-start(bf16[1,64,256]{2,1,0:T(8,128)(2,1)S(1)} %get-tuple-element.71), channel_id=1, source_target_pairs={{0,1},{1,2},{2,3},{3,4},{4,5},{5,6},{6,7},{7,8},{8,9},{9,10},{10,1... | collective-permute-start | bytes 98312 | tf_op jit(solution)/shard_map/ppermute | solution.py:10
  132.8 5.5 collective-permute-start.14
  137.2 6.6 collective-permute-start.13
  152.5 11.1 %collective-permute-start.16 = (bf16[1,64,256]{2,1,0:T(8,128)(2,1)S(1)}, bf16[1,64,256]{2,1,0:T(8,128)(2,1)S(1)}, u32[]{:S(2)}, u32[]{:S(2)}) collective-permute-start(bf16[1,64,256]{2,1,0:T(8,128)(2,1)S(1)} %get-tuple-element.67), channel_id=1, source_target_pairs={{0,16},{16,0},{32,48},{48,32},{64,80},{80,64},{96,112},{112,96},{1... | collective-permute-start | bytes 98312 | tf_op jit(solution)/shard_map/ppermute | solution.py:19
  152.5 14.0 %collective-permute-start.15 = (bf16[1,64,256]{2,1,0:T(8,128)(2,1)S(1)}, bf16[1,64,256]{2,1,0:T(8,128)(2,1)S(1)}, u32[]{:S(2)}, u32[]{:S(2)}) collective-permute-start(bf16[1,64,256]{2,1,0:T(8,128)(2,1)S(1)} %get-tuple-element.67), channel_id=1, source_target_pairs={{0,1},{1,2},{2,3},{3,4},{4,5},{5,6},{6,7},{7,8},{8,9},{9,10},{10,1... | collective-permute-start | bytes 98312 | tf_op jit(solution)/shard_map/ppermute | solution.py:10
  159.3 12.3 %collective-permute-start.19 = (bf16[1,64,256]{2,1,0:T(8,128)(2,1)}, bf16[1,64,256]{2,1,0:T(8,128)(2,1)S(1)}, u32[]{:S(2)}, u32[]{:S(2)}) collective-permute-start(bf16[1,64,256]{2,1,0:T(8,128)(2,1)} %get-tuple-element.66), channel_id=1, source_target_pairs={{1,0},{2,1},{3,2},{4,3},{5,4},{6,5},{7,6},{8,7},{9,8},{10,9},{11,1... | collective-permute-start | bytes 98312 | tf_op jit(solution)/shard_map/ppermute | solution.py:10
  171.7 4.8 collective-permute-start.21
  174.4 6.8 collective-permute-start.20
  265.6 16.6 %collective-permute-start.23 = (bf16[3,32,4096]{2,1,0:T(8,128)(2,1)}, bf16[3,32,4096]{2,1,0:T(8,128)(2,1)}, u32[]{:S(2)}, u32[]{:S(2)}) collective-permute-start(bf16[3,32,4096]{2,1,0:T(8,128)(2,1)} %squeeze.110), channel_id=1, source_target_pairs={{1,0},{2,1},{3,2},{4,3},{5,4},{6,5},{7,6},{8,7},{9,8},{10,9},{11,1... | collective-permute-start | bytes 2359304 | tf_op jit(solution)/shard_map/ppermute | solution.py:10
  267.7 15.7 %collective-permute-start.22 = (bf16[3,32,4096]{2,1,0:T(8,128)(2,1)}, bf16[3,32,4096]{2,1,0:T(8,128)(2,1)}, u32[]{:S(2)}, u32[]{:S(2)}) collective-permute-start(bf16[3,32,4096]{2,1,0:T(8,128)(2,1)} %squeeze.109), channel_id=1, source_target_pairs={{0,1},{1,2},{2,3},{3,4},{4,5},{5,6},{6,7},{7,8},{8,9},{9,10},{10,1... | collective-permute-start | bytes 2359304 | tf_op jit(solution)/shard_map/ppermute | solution.py:10
  285.1 26.6 %collective-permute-start.24 = (bf16[3,32,4096]{2,1,0:T(8,128)(2,1)S(1)}, bf16[3,32,4096]{2,1,0:T(8,128)(2,1)S(1)}, u32[]{:S(2)}, u32[]{:S(2)}) collective-permute-start(bf16[3,32,4096]{2,1,0:T(8,128)(2,1)S(1)} %get-tuple-element.30), channel_id=1, source_target_pairs={{0,112},{16,0},{32,16},{48,32},{64,48},{80,64},{96,80},{112,96},{1... | collective-permute-start | bytes 2359304 | tf_op jit(solution)/shard_map/ppermute | solution.py:15
  285.2 39.1 %collective-permute-start.25 = (bf16[3,32,4096]{2,1,0:T(8,128)(2,1)S(1)}, bf16[3,32,4096]{2,1,0:T(8,128)(2,1)S(1)}, u32[]{:S(2)}, u32[]{:S(2)}) collective-permute-start(bf16[3,32,4096]{2,1,0:T(8,128)(2,1)S(1)} %get-tuple-element.31), channel_id=1, source_target_pairs={{0,16},{16,32},{32,48},{48,64},{64,80},{80,96},{96,112},{112,0},{1... | collective-permute-start | bytes 2359304 | tf_op jit(solution)/shard_map/ppermute | solution.py:15
  336.2 348.1 %all-reduce.5.cloned.1.call-start = ((), (), s32[]{:S(2)}) async-start(), calls=%async_computation | async-start | bytes 9699328 | tf_op jit(solution)/shard_map/psum | solution.py:186
  (51 other events, 382.7 us)
Sparse Core Ops, SparseCore 0:
  336.3 214.4 all-reduce.6
  553.8 130.4 all-reduce.4
